TPU v7x, 32 devices: a whole 2x2x4 slice. The times are simulated.
32 devices in a mesh: row: 4 (over y, core), col: 8 (over z, x).
Axes of the slice: x: 2, y: 2, z: 4, core: 2. Of those that a mesh axis runs over, the one named last changes fastest.
Arguments:
- factor: float32 [24, 262144], P(None, ('row', 'col')), may hold values from -1.2 to 1.2
- prior: float32 [24, 262144], P(None, ('row', 'col')), may hold values from -1.2 to 1.2
- tile_src: int32 [32, 384], P(('row', 'col')), may hold values from 0 to 63
- tile_dst: int32 [32, 384], P(('row', 'col')), may hold values from 0 to 63
- tile_count: int32 [32], P(('row', 'col')), may hold values from 96 to 384, as said below
- tile_vals: bfloat16 [12288, 128, 128], P(('row', 'col'))
- sep_idx: int32 [32, 4, 256], P(('row', 'col')), may hold values from 0 to 8191, as said below
- sep_count: int32 [32, 4], P(('row', 'col')), may hold values from 64 to 256, as said below
- couple: bfloat16 [32, 4, 256, 256], P(('row', 'col')), may hold values from -0.1875 to 0.1875
- masks: int32 [4], replicated, may hold values from 1 to 31, as said below
Outputs:
- new_factor: float32 [24, 262144], P(None, ('row', 'col'))
- momentum: float32 [], replicated
- energy: float32 [], replicated
Inputs may be any that keep to these rules, and one draw needn't show every extreme that they name: `tile_count`: some partition has all 384 slots live; slots at or beyond a partition's count are padding. `sep_idx`: distinct within one partition and round. `sep_count`: in every round some partition has all 256 slots live. masks[0] is 31, masks[1] is 16 and the last round's mask is 1.
All inputs are finite; a program needn't handle non-finite values.
Results may differ from a plain program's by a relative error of at most 0.0031.
Values may be sent and summed in bfloat16 or wider, within the bound.
A program may use at most 128 MiB of HBM per device.

v0:
```python
import jax
import jax.numpy as jnp
from jax import lax
from jax.sharding import PartitionSpec as P

TILE = 128
ITERS = 2


MOMENTUM_CAP = 0.9


def swapped(block, axis, distance):
    count = lax.axis_size(axis)
    route = []
    for low in range(count):
        high = low | 1 << distance
        if high != low and high < count:
            route += [(low, high), (high, low)]
    return lax.ppermute(block, axis, route)


def tile_product(packed, sources, targets, tile_vals, live_tiles, block_count):
    grouped = packed.reshape(packed.shape[0], block_count, packed.shape[1] // block_count)
    picked = jnp.take(grouped, sources, axis=1)
    products = jnp.einsum("rtk,tkc->trc", picked, tile_vals, preferred_element_type=jnp.float32)
    products = products * live_tiles[:, None, None]
    summed = jax.ops.segment_sum(products, targets, num_segments=block_count)
    return summed.transpose(1, 0, 2).reshape(packed.shape[0], packed.shape[1])


def local(
    factor, prior, tile_src, tile_dst, tile_count, tile_vals, sep_idx, sep_count, couple, masks
):
    part_count = lax.axis_size(("row", "col"))
    nodes_all = part_count * factor.shape[1]
    block_count = factor.shape[1] // TILE
    slot_count = sep_idx.shape[2]
    round_count = sep_idx.shape[1]
    live_tiles = (jnp.arange(tile_src.shape[1], dtype=jnp.int32) < tile_count[0]).astype(
        jnp.float32
    )
    slot_range = jnp.arange(slot_count, dtype=jnp.int32)
    bit_count = part_count.bit_length() - 1
    current = factor
    previous = prior
    beta = jnp.float32(0.5 * MOMENTUM_CAP)
    energy = jnp.float32(0.0)
    for iterate in range(ITERS):
        blend = current + beta * (current - previous)
        packed = blend.astype(jnp.bfloat16)
        applied = tile_product(packed, tile_src[0], tile_dst[0], tile_vals, live_tiles, block_count)
        sent_list = []
        for rounds in range(round_count):
            picked = jnp.take(packed, sep_idx[0, rounds], axis=1)
            keep = slot_range < sep_count[0, rounds]
            sent_list.append(jnp.where(keep[None, :], picked, jnp.zeros_like(picked)))
        moving_all = jnp.stack(sent_list, axis=0)
        for bit_pos in range(bit_count):
            swapped_all = swapped(moving_all, ("row", "col"), bit_pos)
            use_bits = jnp.right_shift(masks, bit_pos) % 2 == 1
            moving_all = jnp.where(use_bits[:, None, None], swapped_all, moving_all)
        received = [moving_all[rounds] for rounds in range(round_count)]
        for rounds in range(round_count):
            extra = jnp.dot(received[rounds], couple[0, rounds], preferred_element_type=jnp.float32)
            keep = slot_range < sep_count[0, rounds]
            extra = jnp.where(keep[None, :], extra, jnp.zeros_like(extra))
            applied = applied.at[:, sep_idx[0, rounds]].add(extra)
        moved = blend + applied
        length = jnp.sqrt(jnp.sum(moved * moved, axis=0, keepdims=True))
        updated = moved / jnp.maximum(length, 1.0)
        change, total = lax.psum(
            (jnp.sum(applied * (updated - current)), jnp.sum(applied * updated)), ("row", "col")
        )
        energy = total / nodes_all
        beta = MOMENTUM_CAP * 0.5 * (1.0 + jnp.tanh(change / nodes_all))
        previous = current
        current = updated
    return (current, beta, energy)


def solution(mesh):
    in_specs = (
        P(None, ("row", "col")),
        P(None, ("row", "col")),
        P(("row", "col"), None),
        P(("row", "col"), None),
        P(("row", "col")),
        P(("row", "col"), None, None),
        P(("row", "col"), None, None),
        P(("row", "col"), None),
        P(("row", "col"), None, None, None),
        P(),
    )
    out_specs = (P(None, ("row", "col")), P(), P())
    return jax.shard_map(local, mesh=mesh, in_specs=in_specs, out_specs=out_specs, check_vma=False)
```

profile of v0, /device:TPU:0, one launch (start us, length us, event | category | flops | bytes accessed | tf_op | source)
XLA Modules:
  0.0 314.9 jit_solution(88589080483346817)
XLA Ops:
  0.7 3.7 %copy.57 = f32[24,8192]{0,1:T(8,128)} copy(f32[24,8192]{1,0:T(8,128)} %param.15) | data formatting | bytes 1572864 | tf_op args[1]
  4.3 2.7 copy.58
  7.1 4.1 %fusion.15 = bf16[24,8192]{0,1:T(8,128)(2,1)S(1)} fusion(f32[24,8192]{0,1:T(8,128)} %copy.58, f32[24,8192]{0,1:T(8,128)} %copy.57), kind=kLoop, calls=%fused_computation.42 | loop fusion | flops 786432 | bytes 1966080 | tf_op jit(solution)/shard_map/convert_element_type | solution.py:51
  18.4 3.0 collective-permute-start
  27.9 3.1 collective-permute-start.2
  31.8 2.3 gather_fusion
  34.2 8.7 %broadcast_multiply_fusion.1 = f32[384,24,128]{2,1,0:T(8,128)} fusion(f32[384]{0:T(512)S(1)} %get-tuple-element.41, bf16[384,128,128]{2,1,0:T(8,128)(2,1)} %param.19, bf16[384,24,128]{2,1,0:T(8,128)(2,1)S(1)} %gather_fusion, pred[384]{0:T(512)(128)(4,1)S(1)} %get-tuple-element.42), kind=kOutput, calls=%fused_computation.34 | convolution fusion | flops 304349184 | bytes 19662720 | tf_op jit(solution)/shard_map/rtk,tkc->trc/dot_general | solution.py:26
  44.7 33.1 %scatter_fusion = f32[64,24,128]{2,1,0:T(8,128)S(1)} fusion(f32[64,24,128]{2,1,0:T(8,128)S(1)} %broadcast.147.clone, s32[384]{0:T(512)S(1)} %reduce, f32[384,24,128]{2,1,0:T(8,128)} %broadcast_multiply_fusion.1), kind=kCustom, calls=%fused_computation.10 | custom fusion | flops 1179648 | bytes 14157312 | tf_op jit(solution)/shard_map/scatter-add | solution.py:28
  77.7 2.6 copy.86
  81.5 5.9 %scatter_fusion.1 = f32[24,8192]{0,1:T(8,128)} fusion(f32[24,8192]{0,1:T(8,128)} %bitcast.151, s32[256]{0:T(256)S(1)} %bitcast.160, f32[256,24]{1,0:T(8,128)S(1)} %copy.67), kind=kCustom, calls=%fused_computation.11 | custom fusion | flops 6144 | bytes 74752 | tf_op jit(solution)/shard_map/scatter-add | solution.py:68
  87.3 5.9 %scatter_fusion.2 = f32[24,8192]{0,1:T(8,128)} fusion(f32[24,8192]{0,1:T(8,128)} %scatter_fusion.1, s32[256]{0:T(256)S(1)} %bitcast.158, f32[256,24]{1,0:T(8,128)S(1)} %copy.68), kind=kCustom, calls=%fused_computation.12 | custom fusion | flops 6144 | bytes 74752 | tf_op jit(solution)/shard_map/scatter-add | solution.py:68
  93.2 5.9 %scatter_fusion.3 = f32[24,8192]{0,1:T(8,128)} fusion(f32[24,8192]{0,1:T(8,128)} %scatter_fusion.2, s32[256]{0:T(256)S(1)} %bitcast.156, f32[256,24]{1,0:T(8,128)S(1)} %copy.69), kind=kCustom, calls=%fused_computation.13 | custom fusion | flops 6144 | bytes 74752 | tf_op jit(solution)/shard_map/scatter-add | solution.py:68
  99.1 5.9 %scatter_fusion.4 = f32[24,8192]{0,1:T(8,128)} fusion(f32[24,8192]{0,1:T(8,128)} %scatter_fusion.3, s32[256]{0:T(256)S(1)} %bitcast.154, f32[256,24]{1,0:T(8,128)S(1)} %copy.70), kind=kCustom, calls=%fused_computation.14 | custom fusion | flops 6144 | bytes 74752 | tf_op jit(solution)/shard_map/scatter-add | solution.py:68
  104.9 6.0 %multiply_reduce_fusion.4 = f32[8192]{0:T(1024)S(1)} fusion(f32[24,8192]{0,1:T(8,128)} %scatter_fusion.4, f32[24,8192]{0,1:T(8,128)} %copy.58, f32[24,8192]{0,1:T(8,128)} %copy.57), kind=kLoop, calls=%fused_computation.25 | loop fusion | flops 1171456 | bytes 2392064 | tf_op jit(solution)/shard_map/reduce_sum | solution.py:70
  113.2 6.1 %multiply_reduce_fusion.3 = (f32[]{:T(128)}, f32[24,8192]{0,1:T(8,128)}, f32[24,8192]{0,1:T(8,128)}) fusion(f32[24,8192]{0,1:T(8,128)S(1)} %copy-done.4, f32[24,8192]{0,1:T(8,128)S(1)} %copy-done.1, f32[8192]{0:T(1024)S(1)} %sqrt_maximum_fusion.1, f32[24,8192]{0,1:T(8,128)S(1)} %copy-done), kind=kLoop, calls=%fused_computation.24 | loop fusion | flops 1572863 | bytes 3964932 | tf_op jit(solution)/shard_map/reduce_sum | solution.py:73
  119.4 39.4 %psum.21 = f32[]{:T(128)} all-reduce(f32[]{:T(128)} %get-tuple-element.21), channel_id=1, replica_groups=mesh['row'=4,'col'=8] {'row','col'}, use_global_device_ids=true, to_apply=%region_7.10 | all-reduce | flops 1 | bytes 8 | tf_op jit(solution)/shard_map/psum | solution.py:72
  159.5 3.9 %fusion.13 = bf16[24,8192]{0,1:T(8,128)(2,1)S(1)} fusion(f32[24,8192]{0,1:T(8,128)} %get-tuple-element.23, f32[24,8192]{0,1:T(8,128)} %get-tuple-element.22, f32[]{:T(128)S(6)} %mul.53), kind=kLoop, calls=%fused_computation.40 | loop fusion | flops 589824 | bytes 1966084 | tf_op jit(solution)/shard_map/convert_element_type | solution.py:51
  167.2 2.3 collective-permute-start.5
  173.2 2.6 collective-permute-done.6
  175.9 2.3 collective-permute-start.7
  178.3 2.7 collective-permute-done.7
  186.5 8.7 %broadcast_multiply_fusion = f32[384,24,128]{2,1,0:T(8,128)} fusion(f32[384]{0:T(512)S(1)} %get-tuple-element.41, bf16[384,128,128]{2,1,0:T(8,128)(2,1)} %param.19, bf16[384,24,128]{2,1,0:T(8,128)(2,1)S(1)} %gather_fusion.5, pred[384]{0:T(512)(128)(4,1)S(1)} %get-tuple-element.42), kind=kOutput, calls=%fused_computation.33 | convolution fusion | flops 304349184 | bytes 19662720 | tf_op jit(solution)/shard_map/rtk,tkc->trc/dot_general | solution.py:26
  195.3 33.1 %scatter_fusion.5 = f32[64,24,128]{2,1,0:T(8,128)S(1)} fusion(f32[64,24,128]{2,1,0:T(8,128)S(1)} %broadcast.147, s32[384]{0:T(512)S(1)} %reduce, f32[384,24,128]{2,1,0:T(8,128)} %broadcast_multiply_fusion), kind=kCustom, calls=%fused_computation.15 | custom fusion | flops 1179648 | bytes 14157312 | tf_op jit(solution)/shard_map/scatter-add | solution.py:28
  228.3 2.6 copy.87
  232.0 5.9 %scatter_fusion.6 = f32[24,8192]{0,1:T(8,128)} fusion(f32[24,8192]{0,1:T(8,128)} %bitcast.150, s32[256]{0:T(256)S(1)} %bitcast.161, f32[256,24]{1,0:T(8,128)S(1)} %copy.79), kind=kCustom, calls=%fused_computation.16 | custom fusion | flops 6144 | bytes 74752 | tf_op jit(solution)/shard_map/scatter-add | solution.py:68
  237.9 5.9 %scatter_fusion.7 = f32[24,8192]{0,1:T(8,128)} fusion(f32[24,8192]{0,1:T(8,128)} %scatter_fusion.6, s32[256]{0:T(256)S(1)} %bitcast.159, f32[256,24]{1,0:T(8,128)S(1)} %copy.80), kind=kCustom, calls=%fused_computation.17 | custom fusion | flops 6144 | bytes 74752 | tf_op jit(solution)/shard_map/scatter-add | solution.py:68
  243.8 5.9 %scatter_fusion.8 = f32[24,8192]{0,1:T(8,128)} fusion(f32[24,8192]{0,1:T(8,128)} %scatter_fusion.7, s32[256]{0:T(256)S(1)} %bitcast.157, f32[256,24]{1,0:T(8,128)S(1)} %copy.81), kind=kCustom, calls=%fused_computation.18 | custom fusion | flops 6144 | bytes 74752 | tf_op jit(solution)/shard_map/scatter-add | solution.py:68
  249.6 5.9 %scatter_fusion.9 = f32[24,8192]{0,1:T(8,128)} fusion(f32[24,8192]{0,1:T(8,128)} %scatter_fusion.8, s32[256]{0:T(256)S(1)} %bitcast.155, f32[256,24]{1,0:T(8,128)S(1)} %copy.82), kind=kCustom, calls=%fused_computation.19 | custom fusion | flops 6144 | bytes 74752 | tf_op jit(solution)/shard_map/scatter-add | solution.py:68
  255.5 6.2 %multiply_reduce_fusion.2 = (f32[8192]{0:T(1024)S(1)}, f32[24,8192]{0,1:T(8,128)S(1)}) fusion(f32[24,8192]{0,1:T(8,128)} %scatter_fusion.9, f32[24,8192]{0,1:T(8,128)} %get-tuple-element.23, f32[24,8192]{0,1:T(8,128)} %get-tuple-element.22, f32[]{:T(128)S(6)} %mul.53), kind=kLoop, calls=%fused_computation.22 | loop fusion | flops 974848 | bytes 3178500 | tf_op jit(solution)/shard_map/reduce_sum | solution.py:70
  262.6 5.2 %multiply_reduce_fusion = (f32[]{:T(128)}, f32[]{:T(128)}, f32[24,8192]{0,1:T(8,128)}) fusion(f32[24,8192]{0,1:T(8,128)S(1)} %copy-done.3, f32[24,8192]{0,1:T(8,128)S(1)} %copy-done.2, f32[24,8192]{0,1:T(8,128)S(1)} %get-tuple-element.20, f32[8192]{0:T(1024)S(1)} %sqrt_maximum_fusion), kind=kLoop, calls=%fused_computation.20 | loop fusion | flops 1179646 | bytes 3178504 | tf_op jit(solution)/shard_map/reduce_sum | solution.py:73
  267.9 39.9 %all-reduce = (f32[]{:T(128)}, f32[]{:T(128)}) all-reduce(f32[]{:T(128)} %get-tuple-element.15, f32[]{:T(128)} %get-tuple-element.14), channel_id=1, replica_groups=mesh['row'=4,'col'=8] {'row','col'}, use_global_device_ids=true, to_apply=%region_15.18 | all-reduce | flops 2 | bytes 16 | tf_op jit(solution)/shard_map/psum | solution.py:72
  309.1 3.6 %copy.83 = f32[24,8192]{1,0:T(8,128)} copy(f32[24,8192]{0,1:T(8,128)} %get-tuple-element.18) | data formatting | bytes 1572864
  (118 shorter events, 34.0 us)
Async XLA Ops:
  0.6 3.7 %copy-start.6 = (f32[24,8192]{1,0:T(8,128)S(1)}, f32[24,8192]{1,0:T(8,128)}, u32[]{:S(2)}) copy-start(f32[24,8192]{1,0:T(8,128)} %param.14) | copy-start | bytes 2359300
  0.6 6.4 %copy-start.7 = (s32[1,4,256]{2,1,0:T(4,128)S(1)}, s32[1,4,256]{2,1,0:T(4,128)}, u32[]{:S(2)}) copy-start(s32[1,4,256]{2,1,0:T(4,128)} %param.20) | copy-start | bytes 12292
  7.1 5.0 %copy-start.8 = (s32[1,4]{1,0:T(1,128)S(1)}, s32[1,4]{1,0:T(1,128)}, u32[]{:S(2)}) copy-start(s32[1,4]{1,0:T(1,128)} %param.21) | copy-start | bytes 52
  7.1 15.0 %copy-start.9 = (s32[1,384]{1,0:T(1,128)S(1)}, s32[1,384]{1,0:T(1,128)}, u32[]{:S(2)}) copy-start(s32[1,384]{1,0:T(1,128)} %param.16) | copy-start | bytes 4612
  7.1 15.1 %copy-start.11 = (s32[4]{0:T(128)S(1)}, s32[4]{0:T(128)}, u32[]{:S(2)}) copy-start(s32[4]{0:T(128)} %param.23) | copy-start | bytes 52
  18.4 5.1 %collective-permute-start = (bf16[4,24,256]{2,1,0:T(8,128)(2,1)S(1)}, bf16[4,24,256]{2,1,0:T(8,128)(2,1)S(1)}, u32[]{:S(2)}, u32[]{:S(2)}) collective-permute-start(bf16[4,24,256]{2,1,0:T(8,128)(2,1)S(1)} %pad_maximum_fusion), channel_id=1, source_target_pairs={{0,1},{1,0},{2,3},{3,2},{4,5},{5,4},{6,7},{7,6},{8,9},{9,8},{10,11... | collective-permute-start | bytes 147464 | tf_op jit(solution)/shard_map/ppermute | solution.py:20
  23.6 4.2 %collective-permute-start.1 = (bf16[4,24,256]{2,1,0:T(8,128)(2,1)S(1)}, bf16[4,24,256]{2,1,0:T(8,128)(2,1)S(1)}, u32[]{:S(2)}, u32[]{:S(2)}) collective-permute-start(bf16[4,24,256]{2,1,0:T(8,128)(2,1)S(1)} %broadcast_select_fusion.1), channel_id=1, source_target_pairs={{0,2},{2,0},{1,3},{3,1},{4,6},{6,4},{5,7},{7,5},{8,10},{10,8},{9,1... | collective-permute-start | bytes 147464 | tf_op jit(solution)/shard_map/ppermute | solution.py:20
  27.9 6.2 %collective-permute-start.2 = (bf16[4,24,256]{2,1,0:T(8,128)(2,1)S(1)}, bf16[4,24,256]{2,1,0:T(8,128)(2,1)S(1)}, u32[]{:S(2)}, u32[]{:S(2)}) collective-permute-start(bf16[4,24,256]{2,1,0:T(8,128)(2,1)S(1)} %broadcast_select_fusion.3), channel_id=1, source_target_pairs={{0,4},{4,0},{1,5},{5,1},{2,6},{6,2},{3,7},{7,3},{8,12},{12,8},{9,1... | collective-permute-start | bytes 147464 | tf_op jit(solution)/shard_map/ppermute | solution.py:20
  34.2 8.8 %collective-permute-start.3 = (bf16[4,24,256]{2,1,0:T(8,128)(2,1)S(1)}, bf16[4,24,256]{2,1,0:T(8,128)(2,1)S(1)}, u32[]{:S(2)}, u32[]{:S(2)}) collective-permute-start(bf16[4,24,256]{2,1,0:T(8,128)(2,1)S(1)} %broadcast_select_fusion.5), channel_id=1, source_target_pairs={{0,8},{8,0},{1,9},{9,1},{2,10},{10,2},{3,11},{11,3},{4,12},{12,4},... | collective-permute-start | bytes 147464 | tf_op jit(solution)/shard_map/ppermute | solution.py:20
  34.2 10.4 %copy-start.10 = (s32[1,384]{1,0:T(1,128)S(1)}, s32[1,384]{1,0:T(1,128)}, u32[]{:S(2)}) copy-start(s32[1,384]{1,0:T(1,128)} %param.17) | copy-start | bytes 4612
  43.0 37.3 %collective-permute-start.4 = (bf16[4,24,256]{2,1,0:T(8,128)(2,1)S(1)}, bf16[4,24,256]{2,1,0:T(8,128)(2,1)S(1)}, u32[]{:S(2)}, u32[]{:S(2)}) collective-permute-start(bf16[4,24,256]{2,1,0:T(8,128)(2,1)S(1)} %broadcast_select_fusion.7), channel_id=1, source_target_pairs={{0,16},{16,0},{1,17},{17,1},{2,18},{18,2},{3,19},{19,3},{4,20},{20... | collective-permute-start | bytes 147464 | tf_op jit(solution)/shard_map/ppermute | solution.py:20
  77.7 2.7 copy-start.5
  104.9 6.0 %copy-start = (f32[24,8192]{0,1:T(8,128)S(1)}, f32[24,8192]{0,1:T(8,128)}, u32[]{:S(2)}) copy-start(f32[24,8192]{0,1:T(8,128)} %copy.57) | copy-start | bytes 2359300
  104.9 7.1 %copy-start.1 = (f32[24,8192]{0,1:T(8,128)S(1)}, f32[24,8192]{0,1:T(8,128)}, u32[]{:S(2)}) copy-start(f32[24,8192]{0,1:T(8,128)} %copy.58) | copy-start | bytes 2359300
  104.9 8.3 %copy-start.4 = (f32[24,8192]{0,1:T(8,128)S(1)}, f32[24,8192]{0,1:T(8,128)}, u32[]{:S(2)}) copy-start(f32[24,8192]{0,1:T(8,128)} %scatter_fusion.4) | copy-start | bytes 2359300
  167.2 4.4 %collective-permute-start.5 = (bf16[4,24,256]{2,1,0:T(8,128)(2,1)S(1)}, bf16[4,24,256]{2,1,0:T(8,128)(2,1)S(1)}, u32[]{:S(2)}, u32[]{:S(2)}) collective-permute-start(bf16[4,24,256]{2,1,0:T(8,128)(2,1)S(1)} %pad_maximum_fusion.1), channel_id=1, source_target_pairs={{0,1},{1,0},{2,3},{3,2},{4,5},{5,4},{6,7},{7,6},{8,9},{9,8},{10,11... | collective-permute-start | bytes 147464 | tf_op jit(solution)/shard_map/ppermute | solution.py:20
  171.7 4.1 %collective-permute-start.6 = (bf16[4,24,256]{2,1,0:T(8,128)(2,1)S(1)}, bf16[4,24,256]{2,1,0:T(8,128)(2,1)S(1)}, u32[]{:S(2)}, u32[]{:S(2)}) collective-permute-start(bf16[4,24,256]{2,1,0:T(8,128)(2,1)S(1)} %broadcast_select_fusion), channel_id=1, source_target_pairs={{0,2},{2,0},{1,3},{3,1},{4,6},{6,4},{5,7},{7,5},{8,10},{10,8},{9,1... | collective-permute-start | bytes 147464 | tf_op jit(solution)/shard_map/ppermute | solution.py:20
  175.9 5.1 %collective-permute-start.7 = (bf16[4,24,256]{2,1,0:T(8,128)(2,1)S(1)}, bf16[4,24,256]{2,1,0:T(8,128)(2,1)S(1)}, u32[]{:S(2)}, u32[]{:S(2)}) collective-permute-start(bf16[4,24,256]{2,1,0:T(8,128)(2,1)S(1)} %broadcast_select_fusion.2), channel_id=1, source_target_pairs={{0,4},{4,0},{1,5},{5,1},{2,6},{6,2},{3,7},{7,3},{8,12},{12,8},{9,1... | collective-permute-start | bytes 147464 | tf_op jit(solution)/shard_map/ppermute | solution.py:20
  181.0 3.1 collective-permute-start.8
  184.3 46.7 %collective-permute-start.9 = (bf16[4,24,256]{2,1,0:T(8,128)(2,1)S(1)}, bf16[4,24,256]{2,1,0:T(8,128)(2,1)S(1)}, u32[]{:S(2)}, u32[]{:S(2)}) collective-permute-start(bf16[4,24,256]{2,1,0:T(8,128)(2,1)S(1)} %broadcast_select_fusion.6), channel_id=1, source_target_pairs={{0,16},{16,0},{1,17},{17,1},{2,18},{18,2},{3,19},{19,3},{4,20},{20... | collective-permute-start | bytes 147464 | tf_op jit(solution)/shard_map/ppermute | solution.py:20
  255.5 6.2 %copy-start.2 = (f32[24,8192]{0,1:T(8,128)S(1)}, f32[24,8192]{0,1:T(8,128)}, u32[]{:S(2)}) copy-start(f32[24,8192]{0,1:T(8,128)} %get-tuple-element.23) | copy-start | bytes 2359300
  255.5 7.1 %copy-start.3 = (f32[24,8192]{0,1:T(8,128)S(1)}, f32[24,8192]{0,1:T(8,128)}, u32[]{:S(2)}) copy-start(f32[24,8192]{0,1:T(8,128)} %scatter_fusion.9) | copy-start | bytes 2359300
where the time goes:
time: 317 us; the launch traced here: 315 us
  other arithmetic  148 us (47%)
  blocking collectives  79.3 us (25%)
  local copies, waits for them, and re-layouts  33.6 us (11%)
  matrix products  18.7 us (6%)
  starting transfers between devices  18.2 us (6%)
  waiting for transfers between devices  10.8 us (3%)
  between operations  6.04 us (2%)
    psum x2, blocking collectives, local(): lax.psum((jnp.sum(applied * (updated - current)), jnp.sum(applied * updat...  79.3 us
    scatter-add x2, other arithmetic, tile_product(): summed = jax.ops.segment_sum(products, targets, num_segments=block_count)  66.1 us
    scatter-add x8, other arithmetic, local(): applied = applied.at[:, sep_idx[0, rounds]].add(extra)  46.9 us
    ppermute x10, starting transfers between devices, swapped(): return lax.ppermute(block, axis, route)  18.2 us
    dot_general x2, matrix products, tile_product(): jnp.einsum('rtk,tkc->trc', picked, tile_vals, preferred_element_type=jnp....  17.5 us
    unnamed x27, local copies, waits for them, and re-layouts  13.2 us
    reduce_sum x2, other arithmetic, local(): length = jnp.sqrt(jnp.sum(moved * moved, axis=0, keepdims=True))  12.1 us
    ppermute x10, waiting for transfers between devices, swapped(): return lax.ppermute(block, axis, route)  10.8 us
  transfers between devices with their start and end apart: 10, of which 5 were waited for; matrix products, arithmetic and copies ran while one was open for 30% of the time, Pallas kernels for 0%

commit v1 on v0

v1 whole, which is shorter than its diff:
```python
import functools

import jax
import jax.numpy as jnp
from jax import lax
from jax.experimental import pallas as pl
from jax.experimental.pallas import tpu as pltpu
from jax.sharding import PartitionSpec as P

TILE = 128
ITERS = 2
MOMENTUM_CAP = 0.9
MESH = pl.DeviceIdType.MESH
LIMIT = 60 * 1024 * 1024


def flip(x, j):
    bit = 1
    while bit <= j:
        if j & bit:
            x = x + bit * (1 - 2 * ((x // bit) % 2))
        bit *= 2
    return x


def step_kernel(mode, rows, cols, nodes_all, *refs):
    first, last = mode == "first", mode == "last"
    parts = rows * cols
    refs = list(refs)
    take = lambda n: [refs.pop(0) for _ in range(n)]
    if not last:
        idx_ref, cnt_ref, masks_ref = take(3)
    if first:
        cur_ref, prior_ref = take(2)
    else:
        cur_ref, blend_ref, app_ref = take(3)
    if not first:
        new_ref = take(1)[0]
    if not last:
        nblend_ref, packed_ref, recv_ref = take(3)
    else:
        beta_ref, energy_ref = take(2)
    if not first:
        stat, srow, scol = take(3)
        st_send, st_rrow, st_rcol = take(3)
    if not last:
        xt, gt, sbuf, direct, brow, bcol, picked = take(7)
        d_send, d_recv, c_send, c_recv, r_send, r_recv = take(6)

    comps = cur_ref.shape[0]
    blocks = cur_ref.shape[1] // TILE
    r = lax.axis_index("row")
    c = lax.axis_index("col")

    barrier = pltpu.get_barrier_semaphore()
    peers = [(flip(r, j), c) for j in range(1, rows)] + [(r, flip(c, j)) for j in range(1, cols)]
    if not last:
        peers.append((flip(r, rows - 1), flip(c, cols - 1)))
    for peer in peers:
        pl.semaphore_signal(barrier, inc=1, device_id=peer, device_id_type=MESH)

    def lanes(b):
        return pl.ds(pl.multiple_of(b * TILE, TILE), TILE)

    if first:
        pl.semaphore_wait(barrier, len(peers))
        beta = 0.5 * MOMENTUM_CAP
    else:
        def norm_block(b, carry):
            change, total = carry
            applied = app_ref[:, lanes(b)]
            moved = blend_ref[:, lanes(b)] + applied
            length = jnp.sqrt(jnp.sum(moved * moved, axis=0, keepdims=True))
            updated = moved / jnp.maximum(length, 1.0)
            new_ref[:, lanes(b)] = updated
            return (change + applied * (updated - cur_ref[:, lanes(b)]), total + applied * updated)

        zero = jnp.zeros((comps, TILE), jnp.float32)
        change, total = lax.fori_loop(0, blocks, norm_block, (zero, zero), unroll=4)
        stat[...] = jnp.zeros_like(stat)
        stat[0, 0:1, :] = jnp.sum(change, axis=0, keepdims=True)
        stat[0, 1:2, :] = jnp.sum(total, axis=0, keepdims=True)
        pl.semaphore_wait(barrier, len(peers))
        copies = []
        for j in range(1, rows):
            copies.append(pltpu.make_async_remote_copy(
                src_ref=stat.at[0], dst_ref=srow.at[r], send_sem=st_send.at[j],
                recv_sem=st_rrow.at[r], device_id=(flip(r, j), c), device_id_type=MESH))
        for copy in copies:
            copy.start()
        for j in range(1, rows):
            q = flip(r, j)
            pltpu.make_async_remote_copy(
                src_ref=stat.at[0], dst_ref=srow.at[q], send_sem=st_send.at[j],
                recv_sem=st_rrow.at[q], device_id=(q, c), device_id_type=MESH).wait_recv()
        mine = stat[0]
        both = jnp.where(r == 0, mine, srow[0])
        for q in range(1, rows):
            both = both + jnp.where(r == q, mine, srow[q])
        stat[1] = both
        more = []
        for j in range(1, cols):
            more.append(pltpu.make_async_remote_copy(
                src_ref=stat.at[1], dst_ref=scol.at[c], send_sem=st_send.at[rows + j],
                recv_sem=st_rcol.at[c], device_id=(r, flip(c, j)), device_id_type=MESH))
        for copy in more:
            copy.start()
        for j in range(1, cols):
            q = flip(c, j)
            pltpu.make_async_remote_copy(
                src_ref=stat.at[1], dst_ref=scol.at[q], send_sem=st_send.at[rows + j],
                recv_sem=st_rcol.at[q], device_id=(r, q), device_id_type=MESH).wait_recv()
        both = stat[1]
        every = jnp.where(c == 0, both, scol[0])
        for q in range(1, cols):
            every = every + jnp.where(c == q, both, scol[q])
        sums = jnp.sum(every, axis=1, keepdims=True) / nodes_all
        beta = MOMENTUM_CAP * 0.5 * (1.0 + jnp.tanh(sums[0:1]))
        if last:
            beta_ref[...] = jnp.broadcast_to(beta, beta_ref.shape)
            energy_ref[...] = jnp.broadcast_to(sums[1:2], energy_ref.shape)
        for copy in copies + more:
            copy.wait_send()

    if last:
        return

    rounds, slots = idx_ref.shape

    def blend_block(b, carry):
        if first:
            now, before = cur_ref[:, lanes(b)], prior_ref[:, lanes(b)]
        else:
            now, before = new_ref[:, lanes(b)], cur_ref[:, lanes(b)]
        blend = now + beta * (now - before)
        nblend_ref[:, lanes(b)] = blend
        packed_ref[b] = blend.astype(jnp.bfloat16)
        xt[pl.ds(pl.multiple_of(b * TILE, TILE), TILE), :] = blend.T
        return carry

    lax.fori_loop(0, blocks, blend_block, 0, unroll=2)

    slot_range = lax.broadcasted_iota(jnp.int32, (1, slots), 1)
    GROUP = 16

    def gather_round(k):
        def group(g, carry):
            base = pl.multiple_of(g * GROUP, GROUP)
            for i in range(GROUP):
                gt[pl.ds(base + i, 1), :] = xt[pl.ds(idx_ref[k, base + i], 1), :]
            return carry

        lax.fori_loop(0, slots // GROUP, group, 0)
        moved = gt[...].T
        sbuf[k] = jnp.where(slot_range < cnt_ref[k], moved, 0.0).astype(jnp.bfloat16)

    def fixed(k):
        if k == 0:
            return parts - 1
        if k == 1:
            return parts // 2
        return 1 if k == rounds - 1 else None

    loose = [k for k in range(rounds) if fixed(k) is None]
    firm = [k for k in range(rounds) if fixed(k) is not None]

    def direct_copy(k):
        mask = fixed(k)
        return pltpu.make_async_remote_copy(
            src_ref=sbuf.at[k], dst_ref=direct.at[k], send_sem=d_send.at[k], recv_sem=d_recv.at[k],
            device_id=(flip(r, mask // cols), flip(c, mask % cols)), device_id_type=MESH)

    sends = []
    for n, k in enumerate(loose):
        gather_round(k)
        for j in range(1, cols):
            sends.append(pltpu.make_async_remote_copy(
                src_ref=sbuf.at[k], dst_ref=bcol.at[n, j], send_sem=c_send.at[n, j], recv_sem=c_recv.at[n, j],
                device_id=(r, flip(c, j)), device_id_type=MESH))
            sends[-1].start()
        bcol[n, 0] = sbuf[k]
    for k in firm:
        gather_round(k)
        copy = direct_copy(k)
        copy.start()
    col_sends = list(sends)
    row_sends = []
    for n, k in enumerate(loose):
        for copy in col_sends[n * (cols - 1):(n + 1) * (cols - 1)]:
            copy.wait_recv()
        picked[n] = bcol[n, masks_ref[k] % cols]
        for j in range(1, rows):
            copy = pltpu.make_async_remote_copy(
                src_ref=picked.at[n], dst_ref=brow.at[n, j], send_sem=r_send.at[n, j], recv_sem=r_recv.at[n, j],
                device_id=(flip(r, j), c), device_id_type=MESH)
            copy.start()
            row_sends.append(copy)
        brow[n, 0] = picked[n]
    for n, k in enumerate(loose):
        for copy in row_sends[n * (rows - 1):(n + 1) * (rows - 1)]:
            copy.wait_recv()
        recv_ref[k] = brow[n, masks_ref[k] // cols]
    for k in firm:
        direct_copy(k).wait_recv()
        recv_ref[k] = direct[k]
    for copy in col_sends + row_sends:
        copy.wait_send()
    for k in firm:
        direct_copy(k).wait_send()


def step(mode, rows, cols, nodes_all, cid, smalls, arrays):
    vm = pl.BlockSpec(memory_space=pltpu.VMEM)
    sm = pl.BlockSpec(memory_space=pltpu.SMEM)
    comps, nodes = arrays[0].shape
    f32, bf16 = jnp.float32, jnp.bfloat16
    dma = pltpu.SemaphoreType.DMA
    outs, scratch = [], []
    if mode != "first":
        outs.append(jax.ShapeDtypeStruct((comps, nodes), f32))
        scratch += [pltpu.VMEM((2, 8, TILE), f32), pltpu.VMEM((rows, 8, TILE), f32), pltpu.VMEM((cols, 8, TILE), f32)]
        scratch += [dma((rows + cols,)), dma((rows,)), dma((cols,))]
    if mode != "last":
        rounds, slots = smalls[0].shape
        loose = max(rounds - 3, 1)
        outs.append(jax.ShapeDtypeStruct((comps, nodes), f32))
        outs.append(jax.ShapeDtypeStruct((nodes // TILE, comps, TILE), bf16))
        outs.append(jax.ShapeDtypeStruct((rounds, comps, slots), bf16))
        scratch += [pltpu.VMEM((nodes, comps), f32), pltpu.VMEM((slots, comps), f32)]
        scratch += [pltpu.VMEM((rounds, comps, slots), bf16), pltpu.VMEM((rounds, comps, slots), bf16)]
        scratch += [pltpu.VMEM((loose, rows, comps, slots), bf16), pltpu.VMEM((loose, cols, comps, slots), bf16)]
        scratch += [pltpu.VMEM((loose, comps, slots), bf16)]
        scratch += [dma((rounds,)), dma((rounds,)), dma((loose, cols)), dma((loose, cols)), dma((loose, rows)), dma((loose, rows))]
    else:
        outs += [jax.ShapeDtypeStruct((1, TILE), f32)] * 2
    return pl.pallas_call(
        functools.partial(step_kernel, mode, rows, cols, nodes_all),
        out_shape=outs,
        in_specs=[sm] * len(smalls) + [vm] * len(arrays),
        out_specs=[vm] * len(outs),
        scratch_shapes=scratch,
        compiler_params=pltpu.CompilerParams(collective_id=cid, has_side_effects=True, vmem_limit_bytes=LIMIT),
        name="step_" + mode,
    )(*smalls, *arrays)


def apply_kernel(chunk, src_ref, dst_ref, tcnt_ref, idx_ref, cnt_ref, vals_ref, packed_ref, recv_ref, couple_ref, out_ref, acc, at, ext):
    pid = pl.program_id(0)
    blocks, comps, _ = packed_ref.shape
    rounds, slots = idx_ref.shape

    @pl.when(pid == 0)
    def _():
        acc[...] = jnp.zeros_like(acc)

    UN = 8

    def group(g, carry):
        prods = []
        for i in range(UN):
            t = g * UN + i
            prods.append(jnp.dot(packed_ref[src_ref[0, pid * chunk + t]], vals_ref[t], preferred_element_type=jnp.float32))
        for i in range(UN):
            t = pid * chunk + g * UN + i
            d = jnp.where(t < tcnt_ref[0], dst_ref[0, t], blocks)
            acc[d] += prods[i]
        return carry

    lax.fori_loop(0, chunk // UN, group, 0)

    @pl.when(pid == pl.num_programs(0) - 1)
    def _():
        at[...] = jnp.zeros_like(at)
        slot_range = lax.broadcasted_iota(jnp.int32, (1, slots), 1)
        for k in range(rounds):
            extra = jnp.dot(recv_ref[k], couple_ref[k], preferred_element_type=jnp.float32)
            ext[...] = jnp.where(slot_range < cnt_ref[k], extra, 0.0).T
            GROUP = 16

            def scatter(g, carry):
                base = pl.multiple_of(g * GROUP, GROUP)
                where = [idx_ref[k, base + i] for i in range(GROUP)]
                sums = [at[pl.ds(where[i], 1), :] + ext[pl.ds(base + i, 1), :] for i in range(GROUP)]
                for i in range(GROUP):
                    at[pl.ds(where[i], 1), :] = sums[i]
                return carry

            lax.fori_loop(0, slots // GROUP, scatter, 0)

        def finish(b, carry):
            span = pl.ds(pl.multiple_of(b * TILE, TILE), TILE)
            out_ref[:, span] = acc[b] + at[span, :].T
            return carry

        lax.fori_loop(0, blocks, finish, 0, unroll=2)


def apply_all(tile_src, tile_dst, tile_count, sep_idx, sep_count, tile_vals, packed, recv, couple):
    tiles = tile_vals.shape[0]
    chunk = 32 if tiles % 32 == 0 else 8
    blocks, comps, _ = packed.shape
    rounds, slots = sep_idx.shape
    nodes = blocks * TILE
    f32 = jnp.float32
    whole = lambda shape: pl.BlockSpec(shape, lambda i, *_: (0,) * len(shape))
    return pl.pallas_call(
        functools.partial(apply_kernel, chunk),
        out_shape=jax.ShapeDtypeStruct((comps, nodes), f32),
        grid_spec=pltpu.PrefetchScalarGridSpec(
            num_scalar_prefetch=5,
            grid=(tiles // chunk,),
            in_specs=[
                pl.BlockSpec((chunk, TILE, TILE), lambda i, *_: (i, 0, 0)),
                whole(packed.shape), whole(recv.shape), whole(couple.shape),
            ],
            out_specs=whole((comps, nodes)),
            scratch_shapes=[
                pltpu.VMEM((blocks + 1, comps, TILE), f32),
                pltpu.VMEM((nodes, comps), f32),
                pltpu.VMEM((slots, comps), f32),
            ],
        ),
        compiler_params=pltpu.CompilerParams(dimension_semantics=("arbitrary",), vmem_limit_bytes=LIMIT),
        name="apply_all",
    )(tile_src, tile_dst, tile_count, sep_idx, sep_count, tile_vals, packed, recv, couple)


def local(rows, cols, factor, prior, tile_src, tile_dst, tile_count, tile_vals, sep_idx, sep_count, couple, masks):
    nodes_all = rows * cols * factor.shape[1]
    smalls = (sep_idx[0], sep_count[0], masks)
    blend, packed, recv = step("first", rows, cols, nodes_all, 0, smalls, (factor, prior))
    current = factor
    for iterate in range(ITERS):
        applied = apply_all(tile_src, tile_dst, tile_count, sep_idx[0], sep_count[0], tile_vals, packed, recv, couple[0])
        if iterate < ITERS - 1:
            current, blend, packed, recv = step("middle", rows, cols, nodes_all, 1 + iterate, smalls, (current, blend, applied))
    current, beta, energy = step("last", rows, cols, nodes_all, ITERS, (), (current, blend, applied))
    return (current, beta[0, 0], energy[0, 0])


def solution(mesh):
    rows, cols = mesh.shape["row"], mesh.shape["col"]
    in_specs = (
        P(None, ("row", "col")),
        P(None, ("row", "col")),
        P(("row", "col"), None),
        P(("row", "col"), None),
        P(("row", "col")),
        P(("row", "col"), None, None),
        P(("row", "col"), None, None),
        P(("row", "col"), None),
        P(("row", "col"), None, None, None),
        P(),
    )
    out_specs = (P(None, ("row", "col")), P(), P())
    return jax.shard_map(functools.partial(local, rows, cols), mesh=mesh, in_specs=in_specs, out_specs=out_specs, check_vma=False)
```

time: 317 us -> 109 us (0.34)
  other arithmetic: 148 us -> 0 us
  Pallas kernels: 0 us -> 101 us
  blocking collectives: 79.3 us -> 0 us
  local copies, waits for them, and re-layouts: 33.6 us -> 2.06 us
  matrix products: 18.7 us -> 0 us
  starting transfers between devices: 18.2 us -> 0 us
  waiting for transfers between devices: 10.8 us -> 0 us
    scatter-add x10 -> x0, other arithmetic: 113 us -> none  [the longest x2 66.1 us: tile_product(): summed = jax.ops.segment_sum(products, targets, num_segments=block_count)]
    pallas_call x0 -> x5, Pallas kernels: none -> 101 us  [the longest x3 57.8 us: step(): pl.pallas_call(functools.partial(step_kernel, mode, rows, cols, nodes_all...]
    psum x2 -> x0, blocking collectives: 79.3 us -> none  [local(): lax.psum((jnp.sum(applied * (updated - current)), jnp.sum(applied * updat...]
    reduce_sum x4 -> x0, other arithmetic: 23.5 us -> none  [the longest x2 12.1 us: local(): length = jnp.sqrt(jnp.sum(moved * moved, axis=0, keepdims=True))]
    dot_general x10 -> x0, matrix products: 18.7 us -> none  [the longest x2 17.5 us: tile_product(): jnp.einsum('rtk,tkc->trc', picked, tile_vals, preferred_element_type=jnp....]
    ppermute x10 -> x0, starting transfers between devices: 18.2 us -> none  [swapped(): return lax.ppermute(block, axis, route)]
    gather x18 -> x0, local copies, waits for them, and re-layouts: 11.9 us -> none  [the longest x16 7.36 us: local(): picked = jnp.take(packed, sep_idx[0, rounds], axis=1)]
    unnamed x27 -> x1, local copies, waits for them, and re-layouts: 13.2 us -> 2.06 us
  transfers between devices with their start and end apart: 10 -> 0, of which waited for: 5 -> 0; matrix products, arithmetic and copies ran while one was open for 30% -> 0% of each run, Pallas kernels for 0% -> 0%
where the time goes in v1:
time: 109 us; the launch traced here: 108 us
  Pallas kernels  101 us (93%)
  between operations  4.79 us (4%)
  local copies, waits for them, and re-layouts  2.06 us (2%)
    pallas_call x3, Pallas kernels, step(): pl.pallas_call(functools.partial(step_kernel, mode, rows, cols, nodes_all...  57.8 us
    pallas_call x2, Pallas kernels, apply_all(): pl.pallas_call(functools.partial(apply_kernel, chunk), out_shape=jax.Shap...  43.1 us

profile of v1, /device:TPU:0, one launch (start us, length us, event | category | flops | bytes accessed | tf_op | source)
XLA Modules:
  0.0 107.8 jit_solution(3885425941495523662)
XLA Ops:
  1.3 19.5 %step_first.1 = (f32[24,8192]{1,0:T(8,128)}, bf16[64,24,128]{2,1,0:T(8,128)(2,1)}, bf16[4,24,256]{2,1,0:T(8,128)(2,1)}) custom-call(s32[4,256]{1,0:T(4,128)} %bitcast.9, s32[4]{0:T(128)} %bitcast.13, s32[4]{0:T(128)} %refs_2_.3, f32[24,8192]{1,0:T(8,128)} %refs_3_.3, f32[24,8192]{1,0:T(8,128)} %refs_4_.1), custom_call_target="tpu_custom_call" | custom-call | tf_op jit(solution)/shard_map/step_first/pallas_call | solution.py:236
  20.8 21.6 %apply_all.2.refs_5_ = f32[24,8192]{1,0:T(8,128)} custom-call(s32[1,384]{1,0:T(1,128)} %src_ref.3, s32[1,384]{1,0:T(1,128)} %dst_ref.3, s32[1]{0:T(128)S(6)} %copy.16.tcnt_ref, s32[4,256]{1,0:T(4,128)} %bitcast.10, s32[4]{0:T(128)} %bitcast.14, bf16[384,128,128]{2,1,0:T(8,128)(2,1)} %vals_ref.3, bf16[64,24,128]{2,1,0:T(8,128)(2,1)} %get-tuple-element.14.packed_ref, ...), custom_call_target="tpu_custom_call" | custom-call | tf_op jit(solution)/shard_map/apply_all/pallas_call | solution.py:306
  42.4 26.6 %step_middle.1 = (f32[24,8192]{1,0:T(8,128)}, f32[24,8192]{1,0:T(8,128)}, bf16[64,24,128]{2,1,0:T(8,128)(2,1)}, bf16[4,24,256]{2,1,0:T(8,128)(2,1)}) custom-call(s32[4,256]{1,0:T(4,128)} %bitcast.11, s32[4]{0:T(128)} %bitcast.15, s32[4]{0:T(128)} %refs_2_.3, f32[24,8192]{1,0:T(8,128)} %refs_3_.3, f32[24,8192]{1,0:T(8,128)} %get-tuple-element.13.refs_4_, ...), custom_call_target="tpu_custom_call" | custom-call | tf_op jit(solution)/shard_map/step_middle/pallas_call | solution.py:236
  68.9 21.6 %apply_all.3.refs_2_ = f32[24,8192]{1,0:T(8,128)} custom-call(s32[1,384]{1,0:T(1,128)} %src_ref.3, s32[1,384]{1,0:T(1,128)} %dst_ref.3, s32[1]{0:T(128)S(6)} %copy.16.tcnt_ref, s32[4,256]{1,0:T(4,128)} %bitcast.12, s32[4]{0:T(128)} %bitcast.16, bf16[384,128,128]{2,1,0:T(8,128)(2,1)} %vals_ref.3, bf16[64,24,128]{2,1,0:T(8,128)(2,1)} %get-tuple-element.18.packed_ref, ...), custom_call_target="tpu_custom_call" | custom-call | tf_op jit(solution)/shard_map/apply_all/pallas_call | solution.py:306
  90.5 11.8 %step_last.1 = (f32[24,8192]{1,0:T(8,128)}, f32[1,128]{1,0:T(1,128)}, f32[1,128]{1,0:T(1,128)}) custom-call(f32[24,8192]{1,0:T(8,128)} %get-tuple-element.16.refs_0_, f32[24,8192]{1,0:T(8,128)} %get-tuple-element.17.refs_1_, f32[24,8192]{1,0:T(8,128)} %apply_all.3.refs_2_), custom_call_target="tpu_custom_call" | custom-call | tf_op jit(solution)/shard_map/step_last/pallas_call | solution.py:236
  102.3 2.1 %copy.17 = f32[24,8192]{1,0:T(8,128)} copy(f32[24,8192]{1,0:T(8,128)} %get-tuple-element.26) | data formatting | bytes 1572864

commit v2 on v1

--- a/solution.py
+++ b/solution.py
@@ -12,6 +12,8 @@
 MOMENTUM_CAP = 0.9
 MESH = pl.DeviceIdType.MESH
 LIMIT = 60 * 1024 * 1024
+UNROLL = 8
+GROUP = 32
 
 
 def flip(x, j):
@@ -32,9 +34,10 @@
         idx_ref, cnt_ref, masks_ref = take(3)
     if first:
         cur_ref, prior_ref = take(2)
+    elif last:
+        part_ref = take(1)[0]
     else:
         cur_ref, blend_ref, app_ref = take(3)
-    if not first:
         new_ref = take(1)[0]
     if not last:
         nblend_ref, packed_ref, recv_ref = take(3)
@@ -47,8 +50,9 @@
         xt, gt, sbuf, direct, brow, bcol, picked = take(7)
         d_send, d_recv, c_send, c_recv, r_send, r_recv = take(6)
 
-    comps = cur_ref.shape[0]
-    blocks = cur_ref.shape[1] // TILE
+    if not last:
+        comps = cur_ref.shape[0]
+        blocks = cur_ref.shape[1] // TILE
     r = lax.axis_index("row")
     c = lax.axis_index("col")
 
@@ -66,20 +70,23 @@
         pl.semaphore_wait(barrier, len(peers))
         beta = 0.5 * MOMENTUM_CAP
     else:
-        def norm_block(b, carry):
-            change, total = carry
-            applied = app_ref[:, lanes(b)]
-            moved = blend_ref[:, lanes(b)] + applied
-            length = jnp.sqrt(jnp.sum(moved * moved, axis=0, keepdims=True))
-            updated = moved / jnp.maximum(length, 1.0)
-            new_ref[:, lanes(b)] = updated
-            return (change + applied * (updated - cur_ref[:, lanes(b)]), total + applied * updated)
-
-        zero = jnp.zeros((comps, TILE), jnp.float32)
-        change, total = lax.fori_loop(0, blocks, norm_block, (zero, zero), unroll=4)
-        stat[...] = jnp.zeros_like(stat)
-        stat[0, 0:1, :] = jnp.sum(change, axis=0, keepdims=True)
-        stat[0, 1:2, :] = jnp.sum(total, axis=0, keepdims=True)
+        if not last:
+            def norm_block(b, carry):
+                change, total = carry
+                applied = app_ref[:, lanes(b)]
+                moved = blend_ref[:, lanes(b)] + applied
+                length = jnp.sqrt(jnp.sum(moved * moved, axis=0, keepdims=True))
+                updated = moved / jnp.maximum(length, 1.0)
+                new_ref[:, lanes(b)] = updated
+                return (change + applied * (updated - cur_ref[:, lanes(b)]), total + applied * updated)
+
+            zero = jnp.zeros((comps, TILE), jnp.float32)
+            change, total = lax.fori_loop(0, blocks, norm_block, (zero, zero), unroll=4)
+            stat[...] = jnp.zeros_like(stat)
+            stat[0, 0:1, :] = jnp.sum(change, axis=0, keepdims=True)
+            stat[0, 1:2, :] = jnp.sum(total, axis=0, keepdims=True)
+        else:
+            stat[0] = part_ref[...]
         pl.semaphore_wait(barrier, len(peers))
         copies = []
         for j in range(1, rows):
@@ -138,19 +145,12 @@
         xt[pl.ds(pl.multiple_of(b * TILE, TILE), TILE), :] = blend.T
         return carry
 
-    lax.fori_loop(0, blocks, blend_block, 0, unroll=2)
+    lax.fori_loop(0, blocks, blend_block, 0, unroll=4)
 
     slot_range = lax.broadcasted_iota(jnp.int32, (1, slots), 1)
-    GROUP = 16
-
     def gather_round(k):
-        def group(g, carry):
-            base = pl.multiple_of(g * GROUP, GROUP)
-            for i in range(GROUP):
-                gt[pl.ds(base + i, 1), :] = xt[pl.ds(idx_ref[k, base + i], 1), :]
-            return carry
-
-        lax.fori_loop(0, slots // GROUP, group, 0)
+        for j in range(slots):
+            gt[j:j + 1, :] = xt[pl.ds(idx_ref[k, j], 1), :]
         moved = gt[...].T
         sbuf[k] = jnp.where(slot_range < cnt_ref[k], moved, 0.0).astype(jnp.bfloat16)
 
@@ -217,7 +217,8 @@
     dma = pltpu.SemaphoreType.DMA
     outs, scratch = [], []
     if mode != "first":
-        outs.append(jax.ShapeDtypeStruct((comps, nodes), f32))
+        if mode != "last":
+            outs.append(jax.ShapeDtypeStruct((comps, nodes), f32))
         scratch += [pltpu.VMEM((2, 8, TILE), f32), pltpu.VMEM((rows, 8, TILE), f32), pltpu.VMEM((cols, 8, TILE), f32)]
         scratch += [dma((rows + cols,)), dma((rows,)), dma((cols,))]
     if mode != "last":
@@ -244,7 +245,11 @@
     )(*smalls, *arrays)
 
 
-def apply_kernel(chunk, src_ref, dst_ref, tcnt_ref, idx_ref, cnt_ref, vals_ref, packed_ref, recv_ref, couple_ref, out_ref, acc, at, ext):
+def apply_kernel(chunk, last, src_ref, dst_ref, tcnt_ref, idx_ref, cnt_ref, vals_ref, packed_ref, recv_ref, couple_ref, *refs):
+    if last:
+        cur_ref, blend_ref, out_ref, stat_ref, acc, at, ext = refs
+    else:
+        out_ref, acc, at, ext = refs
     pid = pl.program_id(0)
     blocks, comps, _ = packed_ref.shape
     rounds, slots = idx_ref.shape
@@ -253,20 +258,13 @@
     def _():
         acc[...] = jnp.zeros_like(acc)
 
-    UN = 8
-
-    def group(g, carry):
+    for base in range(0, chunk, UNROLL):
         prods = []
-        for i in range(UN):
-            t = g * UN + i
-            prods.append(jnp.dot(packed_ref[src_ref[0, pid * chunk + t]], vals_ref[t], preferred_element_type=jnp.float32))
-        for i in range(UN):
-            t = pid * chunk + g * UN + i
-            d = jnp.where(t < tcnt_ref[0], dst_ref[0, t], blocks)
-            acc[d] += prods[i]
-        return carry
-
-    lax.fori_loop(0, chunk // UN, group, 0)
+        for t in range(base, base + UNROLL):
+            prods.append(jnp.dot(packed_ref[src_ref[pid, t]], vals_ref[t], preferred_element_type=jnp.float32))
+        for t in range(base, base + UNROLL):
+            d = jnp.where(pid * chunk + t < tcnt_ref[0], dst_ref[pid, t], blocks)
+            acc[d] += prods[t - base]
 
     @pl.when(pid == pl.num_programs(0) - 1)
     def _():
@@ -275,45 +273,60 @@
         for k in range(rounds):
             extra = jnp.dot(recv_ref[k], couple_ref[k], preferred_element_type=jnp.float32)
             ext[...] = jnp.where(slot_range < cnt_ref[k], extra, 0.0).T
-            GROUP = 16
-
-            def scatter(g, carry):
-                base = pl.multiple_of(g * GROUP, GROUP)
+            for base in range(0, slots, GROUP):
                 where = [idx_ref[k, base + i] for i in range(GROUP)]
-                sums = [at[pl.ds(where[i], 1), :] + ext[pl.ds(base + i, 1), :] for i in range(GROUP)]
+                sums = [at[pl.ds(where[i], 1), :] + ext[base + i:base + i + 1, :] for i in range(GROUP)]
                 for i in range(GROUP):
                     at[pl.ds(where[i], 1), :] = sums[i]
+
+        def applied_at(b):
+            span = pl.ds(pl.multiple_of(b * TILE, TILE), TILE)
+            return span, acc[b] + at[span, :].T
+
+        if not last:
+            def finish(b, carry):
+                span, applied = applied_at(b)
+                out_ref[:, span] = applied
                 return carry
 
-            lax.fori_loop(0, slots // GROUP, scatter, 0)
-
-        def finish(b, carry):
-            span = pl.ds(pl.multiple_of(b * TILE, TILE), TILE)
-            out_ref[:, span] = acc[b] + at[span, :].T
-            return carry
-
-        lax.fori_loop(0, blocks, finish, 0, unroll=2)
-
-
-def apply_all(tile_src, tile_dst, tile_count, sep_idx, sep_count, tile_vals, packed, recv, couple):
+            lax.fori_loop(0, blocks, finish, 0, unroll=4)
+        else:
+            def finish(b, carry):
+                change, total = carry
+                span, applied = applied_at(b)
+                moved = blend_ref[:, span] + applied
+                length = jnp.sqrt(jnp.sum(moved * moved, axis=0, keepdims=True))
+                updated = moved / jnp.maximum(length, 1.0)
+                out_ref[:, span] = updated
+                return (change + applied * (updated - cur_ref[:, span]), total + applied * updated)
+
+            zero = jnp.zeros((comps, TILE), jnp.float32)
+            change, total = lax.fori_loop(0, blocks, finish, (zero, zero), unroll=4)
+            stat_ref[...] = jnp.zeros_like(stat_ref)
+            stat_ref[0:1, :] = jnp.sum(change, axis=0, keepdims=True)
+            stat_ref[1:2, :] = jnp.sum(total, axis=0, keepdims=True)
+
+
+def apply_all(tile_src, tile_dst, tile_count, sep_idx, sep_count, tile_vals, packed, recv, couple, extras=()):
     tiles = tile_vals.shape[0]
     chunk = 32 if tiles % 32 == 0 else 8
     blocks, comps, _ = packed.shape
     rounds, slots = sep_idx.shape
     nodes = blocks * TILE
+    outs = [(comps, nodes), (8, TILE)] if extras else [(comps, nodes)]
     f32 = jnp.float32
     whole = lambda shape: pl.BlockSpec(shape, lambda i, *_: (0,) * len(shape))
     return pl.pallas_call(
-        functools.partial(apply_kernel, chunk),
-        out_shape=jax.ShapeDtypeStruct((comps, nodes), f32),
+        functools.partial(apply_kernel, chunk, bool(extras)),
+        out_shape=[jax.ShapeDtypeStruct(o, f32) for o in outs],
         grid_spec=pltpu.PrefetchScalarGridSpec(
             num_scalar_prefetch=5,
             grid=(tiles // chunk,),
             in_specs=[
                 pl.BlockSpec((chunk, TILE, TILE), lambda i, *_: (i, 0, 0)),
                 whole(packed.shape), whole(recv.shape), whole(couple.shape),
-            ],
-            out_specs=whole((comps, nodes)),
+            ] + [whole(e.shape) for e in extras],
+            out_specs=[whole(o) for o in outs],
             scratch_shapes=[
                 pltpu.VMEM((blocks + 1, comps, TILE), f32),
                 pltpu.VMEM((nodes, comps), f32),
@@ -322,7 +335,7 @@
         ),
         compiler_params=pltpu.CompilerParams(dimension_semantics=("arbitrary",), vmem_limit_bytes=LIMIT),
         name="apply_all",
-    )(tile_src, tile_dst, tile_count, sep_idx, sep_count, tile_vals, packed, recv, couple)
+    )(tile_src.reshape(tiles // chunk, chunk), tile_dst.reshape(tiles // chunk, chunk), tile_count, sep_idx, sep_count, tile_vals, packed, recv, couple, *extras)
 
 
 def local(rows, cols, factor, prior, tile_src, tile_dst, tile_count, tile_vals, sep_idx, sep_count, couple, masks):
@@ -331,10 +344,12 @@
     blend, packed, recv = step("first", rows, cols, nodes_all, 0, smalls, (factor, prior))
     current = factor
     for iterate in range(ITERS):
-        applied = apply_all(tile_src, tile_dst, tile_count, sep_idx[0], sep_count[0], tile_vals, packed, recv, couple[0])
-        if iterate < ITERS - 1:
-            current, blend, packed, recv = step("middle", rows, cols, nodes_all, 1 + iterate, smalls, (current, blend, applied))
-    current, beta, energy = step("last", rows, cols, nodes_all, ITERS, (), (current, blend, applied))
+        final = iterate == ITERS - 1
+        result = apply_all(tile_src, tile_dst, tile_count, sep_idx[0], sep_count[0], tile_vals, packed, recv, couple[0], (current, blend) if final else ())
+        if not final:
+            current, blend, packed, recv = step("middle", rows, cols, nodes_all, 1 + iterate, smalls, (current, blend, *result))
+    current, stat = result
+    beta, energy = step("last", rows, cols, nodes_all, ITERS, (), (stat,))
     return (current, beta[0, 0], energy[0, 0])
 
 

time: 109 us -> 95 us (0.87)
  Pallas kernels: 101 us -> 86.7 us
  other arithmetic: 0 us -> 1.4 us
    pallas_call x2, Pallas kernels: 43.1 us -> 33.4 us  [apply_all(): pl.pallas_call(functools.partial(apply_kernel, chunk, bool(extras)), out_...]
    pallas_call x3, Pallas kernels: 57.8 us -> 53.3 us  [step(): pl.pallas_call(functools.partial(step_kernel, mode, rows, cols, nodes_all...]
    unnamed x1 -> x0, local copies, waits for them, and re-layouts: 2.06 us -> none
    unnamed x0 -> x2, other arithmetic: none -> 1.4 us
    reshape x0 -> x2, local copies, waits for them, and re-layouts: none -> 1.33 us  [the longest x1 0.67 us: apply_all(): tile_dst.reshape(tiles // chunk, chunk)]
where the time goes in v2:
time: 95 us; the launch traced here: 94.2 us
  Pallas kernels  86.7 us (91%)
  between operations  4.8 us (5%)
  other arithmetic  1.4 us (1%)
  local copies, waits for them, and re-layouts  1.33 us (1%)
    pallas_call x3, Pallas kernels, step(): pl.pallas_call(functools.partial(step_kernel, mode, rows, cols, nodes_all...  53.3 us
    pallas_call x2, Pallas kernels, apply_all(): pl.pallas_call(functools.partial(apply_kernel, chunk, bool(extras)), out_...  33.4 us

profile of v2, /device:TPU:0, one launch (start us, length us, event | category | flops | bytes accessed | tf_op | source)
XLA Modules:
  0.0 94.2 jit_solution(5978435874696001172)
XLA Ops:
  1.3 0.7 reduce
  2.0 0.7 reduce.1
  2.7 0.7 reshape.15.dst_ref
  3.3 0.7 reshape.14.src_ref
  4.0 17.8 %step_first.1 = (f32[24,8192]{1,0:T(8,128)}, bf16[64,24,128]{2,1,0:T(8,128)(2,1)}, bf16[4,24,256]{2,1,0:T(8,128)(2,1)}) custom-call(s32[4,256]{1,0:T(4,128)} %bitcast.9, s32[4]{0:T(128)} %bitcast.13, s32[4]{0:T(128)} %refs_2_.3, f32[24,8192]{1,0:T(8,128)} %refs_3_.3, f32[24,8192]{1,0:T(8,128)} %refs_4_.1), custom_call_target="tpu_custom_call" | custom-call | tf_op jit(solution)/shard_map/step_first/pallas_call | solution.py:237
  21.8 16.2 %apply_all.2.refs_5_ = f32[24,8192]{1,0:T(8,128)} custom-call(s32[12,32]{1,0:T(8,128)} %reshape.14.src_ref, s32[12,32]{1,0:T(8,128)} %reshape.15.dst_ref, s32[1]{0:T(128)S(6)} %copy.15.tcnt_ref, s32[4,256]{1,0:T(4,128)} %bitcast.10, s32[4]{0:T(128)} %bitcast.14, bf16[384,128,128]{2,1,0:T(8,128)(2,1)} %vals_ref.3, ...), custom_call_target="tpu_custom_call" | custom-call | tf_op jit(solution)/shard_map/apply_all/pallas_call | solution.py:319
  38.0 25.1 %step_middle.1 = (f32[24,8192]{1,0:T(8,128)}, f32[24,8192]{1,0:T(8,128)}, bf16[64,24,128]{2,1,0:T(8,128)(2,1)}, bf16[4,24,256]{2,1,0:T(8,128)(2,1)}) custom-call(s32[4,256]{1,0:T(4,128)} %bitcast.11, s32[4]{0:T(128)} %bitcast.15, s32[4]{0:T(128)} %refs_2_.3, f32[24,8192]{1,0:T(8,128)} %refs_3_.3, f32[24,8192]{1,0:T(8,128)} %get-tuple-element.14.refs_4_, ...), custom_call_target="tpu_custom_call" | custom-call | tf_op jit(solution)/shard_map/step_middle/pallas_call | solution.py:237
  63.0 17.2 %apply_all.3 = (f32[24,8192]{1,0:T(8,128)}, f32[8,128]{1,0:T(8,128)}) custom-call(s32[12,32]{1,0:T(8,128)} %reshape.14.src_ref, s32[12,32]{1,0:T(8,128)} %reshape.15.dst_ref, s32[1]{0:T(128)S(6)} %copy.15.tcnt_ref, s32[4,256]{1,0:T(4,128)} %bitcast.12, s32[4]{0:T(128)} %bitcast.16, bf16[384,128,128]{2,1,0:T(8,128)(2,1)} %vals_ref.3, ...), custom_call_target="tpu_custom_call" | custom-call | tf_op jit(solution)/shard_map/apply_all/pallas_call | solution.py:319
  80.2 10.5 %step_last.1 = (f32[1,128]{1,0:T(1,128)}, f32[1,128]{1,0:T(1,128)}) custom-call(f32[8,128]{1,0:T(8,128)} %get-tuple-element.22.refs_0_), custom_call_target="tpu_custom_call" | custom-call | tf_op jit(solution)/shard_map/step_last/pallas_call | solution.py:237

commit v3 on v2

v3 whole, which is shorter than its diff:
```python
import functools

import jax
import jax.numpy as jnp
from jax import lax
from jax.experimental import pallas as pl
from jax.experimental.pallas import tpu as pltpu
from jax.sharding import PartitionSpec as P

TILE = 128
ITERS = 2
MOMENTUM_CAP = 0.9
MESH = pl.DeviceIdType.MESH
LIMIT = 60 * 1024 * 1024
UNROLL = 8
BANKS = 1
SHIFT = 16
GROUP = 32


def flip(x, j):
    bit = 1
    while bit <= j:
        if j & bit:
            x = x + bit * (1 - 2 * ((x // bit) % 2))
        bit *= 2
    return x


def step_kernel(mode, rows, cols, nodes_all, *refs):
    first, last = mode == "first", mode == "last"
    parts = rows * cols
    refs = list(refs)
    take = lambda n: [refs.pop(0) for _ in range(n)]
    if not last:
        idx_ref, cnt_ref, masks_ref = take(3)
    if first:
        cur_ref, prior_ref = take(2)
    elif last:
        part_ref = take(1)[0]
    else:
        cur_ref, blend_ref, app_ref = take(3)
        new_ref = take(1)[0]
    if not last:
        nblend_ref, recv_ref = take(2)
    else:
        beta_ref, energy_ref = take(2)
    if not first:
        stat, srow, scol = take(3)
        st_send, st_rrow, st_rcol = take(3)
    if not last:
        xt, gt, sbuf, direct, brow, bcol, picked = take(7)
        d_send, d_recv, c_send, c_recv, r_send, r_recv = take(6)

    if not last:
        comps = cur_ref.shape[0]
        blocks = cur_ref.shape[1] // TILE
    r = lax.axis_index("row")
    c = lax.axis_index("col")

    barrier = pltpu.get_barrier_semaphore()
    peers = [(flip(r, j), c) for j in range(1, rows)] + [(r, flip(c, j)) for j in range(1, cols)]
    if not last:
        peers.append((flip(r, rows - 1), flip(c, cols - 1)))
    for peer in peers:
        pl.semaphore_signal(barrier, inc=1, device_id=peer, device_id_type=MESH)

    def lanes(b):
        return pl.ds(pl.multiple_of(b * TILE, TILE), TILE)

    if not last:
        _, rounds, slots = idx_ref.shape
        slot_range = lax.broadcasted_iota(jnp.int32, (1, slots), 1)

        def gather_round(k):
            for j in range(slots):
                gt[j:j + 1, :] = xt[pl.ds(idx_ref[0, k, j], 1), :]
            sbuf[k] = jnp.where(slot_range < cnt_ref[0, k], gt[...].T, 0.0).astype(jnp.bfloat16)

    def first_block(b, carry):
        blend = cur_ref[:, lanes(b)] + beta0 * (cur_ref[:, lanes(b)] - prior_ref[:, lanes(b)])
        nblend_ref[:, lanes(b)] = blend
        xt[lanes(b), :] = blend.T
        return carry

    def norm_block(b, carry):
        change, total = carry
        applied = app_ref[:, lanes(b)]
        moved = blend_ref[:, lanes(b)] + applied
        length = jnp.sqrt(jnp.sum(moved * moved, axis=0, keepdims=True))
        updated = moved / jnp.maximum(length, 1.0)
        delta = updated - cur_ref[:, lanes(b)]
        new_ref[:, lanes(b)] = updated
        xt[lanes(b), :] = jnp.concatenate([updated, delta], axis=0).T
        return (change + applied * delta, total + applied * updated)

    def stat_copy(stage, slot, q):
        src, dst = stat.at[stage], (srow, scol)[stage].at[slot]
        recv = (st_rrow, st_rcol)[stage].at[slot]
        where = (q, c) if stage == 0 else (r, q)
        return src, dst, recv, where

    def stat_send(stage):
        size, mine = ((rows, r), (cols, c))[stage]
        sent = []
        for j in range(1, size):
            src, dst, recv, where = stat_copy(stage, mine, flip(mine, j))
            sent.append(pltpu.make_async_remote_copy(
                src_ref=src, dst_ref=dst, send_sem=st_send.at[stage * rows + j], recv_sem=recv,
                device_id=where, device_id_type=MESH))
            sent[-1].start()
        return sent

    def stat_take(stage):
        size, mine = ((rows, r), (cols, c))[stage]
        for j in range(1, size):
            q = flip(mine, j)
            src, dst, recv, where = stat_copy(stage, q, q)
            pltpu.make_async_remote_copy(
                src_ref=src, dst_ref=dst, send_sem=st_send.at[stage * rows + j], recv_sem=recv,
                device_id=where, device_id_type=MESH).wait_recv()
        own = stat[stage]
        slots_in = (srow, scol)[stage]
        every = jnp.where(mine == 0, own, slots_in[0])
        for q in range(1, size):
            every = every + jnp.where(mine == q, own, slots_in[q])
        return every

    def stat_beta(every):
        sums = jnp.sum(every, axis=1, keepdims=True) / nodes_all
        return MOMENTUM_CAP * 0.5 * (1.0 + jnp.tanh(sums[0:1])), sums[1:2]

    beta0 = 0.5 * MOMENTUM_CAP
    stat_sends = []
    if first:
        lax.fori_loop(0, blocks, first_block, 0, unroll=4)
        pl.semaphore_wait(barrier, len(peers))
    else:
        stat[...] = jnp.zeros_like(stat)
        if last:
            stat[0] = part_ref[...]
        else:
            zero = jnp.zeros((comps, TILE), jnp.float32)
            change, total = lax.fori_loop(0, blocks, norm_block, (zero, zero), unroll=4)
            stat[0, 0:1, :] = jnp.sum(change, axis=0, keepdims=True)
            stat[0, 1:2, :] = jnp.sum(total, axis=0, keepdims=True)
        pl.semaphore_wait(barrier, len(peers))
        stat_sends += stat_send(0)
        if last:
            stat[1] = stat_take(0)
            stat_sends += stat_send(1)
            beta, energy = stat_beta(stat_take(1))
            beta_ref[...] = jnp.broadcast_to(beta, beta_ref.shape)
            energy_ref[...] = jnp.broadcast_to(energy, energy_ref.shape)
            for copy in stat_sends:
                copy.wait_send()
            return

    def fixed(k):
        if k == 0:
            return parts - 1
        if k == 1:
            return parts // 2
        return 1 if k == rounds - 1 else None

    loose = [k for k in range(rounds) if fixed(k) is None]
    firm = [k for k in range(rounds) if fixed(k) is not None]

    def direct_copy(k):
        mask = fixed(k)
        return pltpu.make_async_remote_copy(
            src_ref=sbuf.at[k], dst_ref=direct.at[k], send_sem=d_send.at[k], recv_sem=d_recv.at[k],
            device_id=(flip(r, mask // cols), flip(c, mask % cols)), device_id_type=MESH)

    sends = []
    for n, k in enumerate(loose):
        gather_round(k)
        for j in range(1, cols):
            sends.append(pltpu.make_async_remote_copy(
                src_ref=sbuf.at[k], dst_ref=bcol.at[n, j], send_sem=c_send.at[n, j], recv_sem=c_recv.at[n, j],
                device_id=(r, flip(c, j)), device_id_type=MESH))
            sends[-1].start()
        bcol[n, 0] = sbuf[k]
    if not first:
        stat[1] = stat_take(0)
        stat_sends += stat_send(1)
    for k in firm:
        gather_round(k)
        copy = direct_copy(k)
        copy.start()
    if not first:
        beta, _ = stat_beta(stat_take(1))

        def blend_block(b, carry):
            now = new_ref[:, lanes(b)]
            nblend_ref[:, lanes(b)] = now + beta * (now - cur_ref[:, lanes(b)])
            return carry

        lax.fori_loop(0, blocks, blend_block, 0, unroll=4)

    def taken(block):
        if first:
            return block
        whole = block.astype(jnp.float32)
        return (whole[:comps] + beta * whole[comps:]).astype(jnp.bfloat16)

    col_sends = list(sends)
    row_sends = []
    for n, k in enumerate(loose):
        for copy in col_sends[n * (cols - 1):(n + 1) * (cols - 1)]:
            copy.wait_recv()
        picked[n] = bcol[n, masks_ref[k] % cols]
        for j in range(1, rows):
            copy = pltpu.make_async_remote_copy(
                src_ref=picked.at[n], dst_ref=brow.at[n, j], send_sem=r_send.at[n, j], recv_sem=r_recv.at[n, j],
                device_id=(flip(r, j), c), device_id_type=MESH)
            copy.start()
            row_sends.append(copy)
        brow[n, 0] = picked[n]
    for n, k in enumerate(loose):
        for copy in row_sends[n * (rows - 1):(n + 1) * (rows - 1)]:
            copy.wait_recv()
        recv_ref[k] = taken(brow[n, masks_ref[k] // cols])
    for k in firm:
        direct_copy(k).wait_recv()
        recv_ref[k] = taken(direct[k])
    for copy in stat_sends + col_sends + row_sends:
        copy.wait_send()
    for k in firm:
        direct_copy(k).wait_send()


def step(mode, rows, cols, nodes_all, cid, smalls, arrays):
    vm = pl.BlockSpec(memory_space=pltpu.VMEM)
    sm = pl.BlockSpec(memory_space=pltpu.SMEM)
    comps, nodes = arrays[0].shape
    f32, bf16 = jnp.float32, jnp.bfloat16
    dma = pltpu.SemaphoreType.DMA
    outs, scratch = [], []
    if mode != "first":
        if mode != "last":
            outs.append(jax.ShapeDtypeStruct((comps, nodes), f32))
        scratch += [pltpu.VMEM((2, 8, TILE), f32), pltpu.VMEM((rows, 8, TILE), f32), pltpu.VMEM((cols, 8, TILE), f32)]
        scratch += [dma((rows + cols,)), dma((rows,)), dma((cols,))]
    if mode != "last":
        _, rounds, slots = smalls[0].shape
        loose = max(rounds - 3, 1)
        outs.append(jax.ShapeDtypeStruct((comps, nodes), f32))
        outs.append(jax.ShapeDtypeStruct((rounds, comps, slots), bf16))
        wide = comps if mode == "first" else 2 * comps
        scratch += [pltpu.VMEM((nodes, wide), f32), pltpu.VMEM((slots, wide), f32)]
        scratch += [pltpu.VMEM((rounds, wide, slots), bf16), pltpu.VMEM((rounds, wide, slots), bf16)]
        scratch += [pltpu.VMEM((loose, rows, wide, slots), bf16), pltpu.VMEM((loose, cols, wide, slots), bf16)]
        scratch += [pltpu.VMEM((loose, wide, slots), bf16)]
        scratch += [dma((rounds,)), dma((rounds,)), dma((loose, cols)), dma((loose, cols)), dma((loose, rows)), dma((loose, rows))]
    else:
        outs += [jax.ShapeDtypeStruct((1, TILE), f32)] * 2
    return pl.pallas_call(
        functools.partial(step_kernel, mode, rows, cols, nodes_all),
        out_shape=outs,
        in_specs=[sm] * len(smalls) + [vm] * len(arrays),
        out_specs=[vm] * len(outs),
        scratch_shapes=scratch,
        compiler_params=pltpu.CompilerParams(collective_id=cid, has_side_effects=True, vmem_limit_bytes=LIMIT),
        name="step_" + mode,
    )(*smalls, *arrays)


def apply_kernel(chunk, last, code_ref, idx_ref, cnt_ref, vals_ref, blend_ref, recv_ref, couple_ref, *refs):
    if last:
        cur_ref, out_ref, stat_ref, *acc, at, ext = refs
    else:
        out_ref, *acc, at, ext = refs
    pid = pl.program_id(0)
    comps, nodes = blend_ref.shape
    blocks = nodes // TILE
    _, rounds, slots = idx_ref.shape

    @pl.when(pid == 0)
    def _():
        for bank in acc:
            bank[...] = jnp.zeros_like(bank)

    for base in range(0, chunk, UNROLL):
        prods = []
        for t in range(base, base + UNROLL, 2):
            spots = [pl.ds(pl.multiple_of((code_ref[pid, t + i] & ((1 << SHIFT) - 1)) * TILE, TILE), TILE) for i in range(2)]
            pair = jnp.concatenate([blend_ref[:, spot] for spot in spots], axis=0).astype(jnp.bfloat16)
            side = jnp.concatenate([vals_ref[t], vals_ref[t + 1]], axis=1)
            both = jnp.dot(pair, side, preferred_element_type=jnp.float32)
            prods += [both[:comps, :TILE], both[comps:, TILE:]]
        for t in range(base, base + UNROLL):
            acc[t % BANKS][code_ref[pid, t] >> SHIFT] += prods[t - base]

    @pl.when(pid == pl.num_programs(0) - 1)
    def _():
        at[...] = jnp.zeros_like(at)
        slot_range = lax.broadcasted_iota(jnp.int32, (1, slots), 1)
        for k in range(rounds):
            extra = jnp.dot(recv_ref[k], couple_ref[k], preferred_element_type=jnp.float32)
            ext[...] = jnp.where(slot_range < cnt_ref[0, k], extra, 0.0).T
            for base in range(0, slots, GROUP):
                where = [idx_ref[0, k, base + i] for i in range(GROUP)]
                sums = [at[pl.ds(where[i], 1), :] + ext[base + i:base + i + 1, :] for i in range(GROUP)]
                for i in range(GROUP):
                    at[pl.ds(where[i], 1), :] = sums[i]

        def applied_at(b):
            span = pl.ds(pl.multiple_of(b * TILE, TILE), TILE)
            return span, sum(bank[b] for bank in acc) + at[span, :].T

        if not last:
            def finish(b, carry):
                span, applied = applied_at(b)
                out_ref[:, span] = applied
                return carry

            lax.fori_loop(0, blocks, finish, 0, unroll=4)
        else:
            def finish(b, carry):
                change, total = carry
                span, applied = applied_at(b)
                moved = blend_ref[:, span] + applied
                length = jnp.sqrt(jnp.sum(moved * moved, axis=0, keepdims=True))
                updated = moved / jnp.maximum(length, 1.0)
                out_ref[:, span] = updated
                return (change + applied * (updated - cur_ref[:, span]), total + applied * updated)

            zero = jnp.zeros((comps, TILE), jnp.float32)
            change, total = lax.fori_loop(0, blocks, finish, (zero, zero), unroll=4)
            stat_ref[...] = jnp.zeros_like(stat_ref)
            stat_ref[0:1, :] = jnp.sum(change, axis=0, keepdims=True)
            stat_ref[1:2, :] = jnp.sum(total, axis=0, keepdims=True)


def apply_all(code, sep_idx, sep_count, tile_vals, blend, recv, couple, extras=()):
    tiles = tile_vals.shape[0]
    chunk = code.shape[1]
    comps, nodes = blend.shape
    blocks = nodes // TILE
    _, rounds, slots = sep_idx.shape
    outs = [(comps, nodes), (8, TILE)] if extras else [(comps, nodes)]
    f32 = jnp.float32
    whole = lambda shape: pl.BlockSpec(shape, lambda i, *_: (0,) * len(shape))
    return pl.pallas_call(
        functools.partial(apply_kernel, chunk, bool(extras)),
        out_shape=[jax.ShapeDtypeStruct(o, f32) for o in outs],
        grid_spec=pltpu.PrefetchScalarGridSpec(
            num_scalar_prefetch=3,
            grid=(tiles // chunk,),
            in_specs=[
                pl.BlockSpec((chunk, TILE, TILE), lambda i, *_: (i, 0, 0)),
                whole(blend.shape), whole(recv.shape), whole(couple.shape),
            ] + [whole(e.shape) for e in extras],
            out_specs=[whole(o) for o in outs],
            scratch_shapes=[
                *[pltpu.VMEM((blocks + 1, comps, TILE), f32) for _ in range(BANKS)],
                pltpu.VMEM((nodes, comps), f32),
                pltpu.VMEM((slots, comps), f32),
            ],
        ),
        compiler_params=pltpu.CompilerParams(dimension_semantics=("arbitrary",), vmem_limit_bytes=LIMIT),
        name="apply_all",
    )(code, sep_idx, sep_count, tile_vals, blend, recv, couple, *extras)


def local(rows, cols, factor, prior, tile_src, tile_dst, tile_count, tile_vals, sep_idx, sep_count, couple, masks):
    nodes_all = rows * cols * factor.shape[1]
    smalls = (sep_idx, sep_count, masks)
    tiles, blocks = tile_src.shape[1], factor.shape[1] // TILE
    live = jnp.arange(tiles, dtype=jnp.int32)[None, :] < tile_count[0]
    chunk = 32 if tiles % 32 == 0 else 8
    code = (jnp.where(live, tile_dst, blocks) * (1 << SHIFT) + tile_src).reshape(tiles // chunk, chunk)
    blend, recv = step("first", rows, cols, nodes_all, 0, smalls, (factor, prior))
    current = factor
    for iterate in range(ITERS):
        final = iterate == ITERS - 1
        result = apply_all(code, sep_idx, sep_count, tile_vals, blend, recv, couple[0], (current,) if final else ())
        if not final:
            current, blend, recv = step("middle", rows, cols, nodes_all, 1 + iterate, smalls, (current, blend, *result))
    current, stat = result
    beta, energy = step("last", rows, cols, nodes_all, ITERS, (), (stat,))
    return (current, beta[0, 0], energy[0, 0])


def solution(mesh):
    rows, cols = mesh.shape["row"], mesh.shape["col"]
    in_specs = (
        P(None, ("row", "col")),
        P(None, ("row", "col")),
        P(("row", "col"), None),
        P(("row", "col"), None),
        P(("row", "col")),
        P(("row", "col"), None, None),
        P(("row", "col"), None, None),
        P(("row", "col"), None),
        P(("row", "col"), None, None, None),
        P(),
    )
    out_specs = (P(None, ("row", "col")), P(), P())
    return jax.shard_map(functools.partial(local, rows, cols), mesh=mesh, in_specs=in_specs, out_specs=out_specs, check_vma=False)
```

time: 95 us -> 84.5 us (0.89)
  Pallas kernels: 86.7 us -> 77.6 us
    pallas_call x3, Pallas kernels: 53.3 us -> 45.2 us  [step(): pl.pallas_call(functools.partial(step_kernel, mode, rows, cols, nodes_all...]
    unnamed x2 -> x0, other arithmetic: 1.4 us -> none
    pallas_call x2, Pallas kernels: 33.4 us -> 32.4 us  [apply_all(): pl.pallas_call(functools.partial(apply_kernel, chunk, bool(extras)), out_...]
where the time goes in v3:
time: 84.5 us; the launch traced here: 83.8 us
  Pallas kernels  77.6 us (92%)
  between operations  4.82 us (6%)
    pallas_call x3, Pallas kernels, step(): pl.pallas_call(functools.partial(step_kernel, mode, rows, cols, nodes_all...  45.2 us
    pallas_call x2, Pallas kernels, apply_all(): pl.pallas_call(functools.partial(apply_kernel, chunk, bool(extras)), out_...  32.4 us

profile of v3, /device:TPU:0, one launch (start us, length us, event | category | flops | bytes accessed | tf_op | source)
XLA Modules:
  0.0 83.8 jit_solution(15642768917705834343)
XLA Ops:
  1.3 0.7 fusion.2
  2.0 0.7 reshape.17.code_ref
  2.7 16.8 %step_first.1 = (f32[24,8192]{1,0:T(8,128)}, bf16[4,24,256]{2,1,0:T(8,128)(2,1)}) custom-call(s32[1,4,256]{2,1,0:T(4,128)} %idx_ref.3, s32[1,4]{1,0:T(1,128)} %cnt_ref.3, s32[4]{0:T(128)} %refs_2_.3, f32[24,8192]{1,0:T(8,128)} %refs_3_.3, f32[24,8192]{1,0:T(8,128)} %refs_4_.1), custom_call_target="tpu_custom_call" | custom-call | tf_op jit(solution)/shard_map/step_first/pallas_call | solution.py:258
  19.5 15.8 %apply_all.2.refs_5_ = f32[24,8192]{1,0:T(8,128)} custom-call(s32[12,32]{1,0:T(8,128)} %reshape.17.code_ref, s32[1,4,256]{2,1,0:T(4,128)} %idx_ref.3, s32[1,4]{1,0:T(1,128)} %cnt_ref.3, bf16[384,128,128]{2,1,0:T(8,128)(2,1)} %vals_ref.3, f32[24,8192]{1,0:T(8,128)} %get-tuple-element.12.blend_ref.refs_4_, bf16[4,24,256]{2,1,0:T(8,128)(2,1)} %get-tuple-element.13.recv_ref, ...), custom_call_target="tpu_custom_call" | custom-call | tf_op jit(solution)/shard_map/apply_all/pallas_call | solution.py:345
  35.3 17.8 %step_middle.1 = (f32[24,8192]{1,0:T(8,128)}, f32[24,8192]{1,0:T(8,128)}, bf16[4,24,256]{2,1,0:T(8,128)(2,1)}) custom-call(s32[1,4,256]{2,1,0:T(4,128)} %idx_ref.3, s32[1,4]{1,0:T(1,128)} %cnt_ref.3, s32[4]{0:T(128)} %refs_2_.3, f32[24,8192]{1,0:T(8,128)} %refs_3_.3, f32[24,8192]{1,0:T(8,128)} %get-tuple-element.12.blend_ref.refs_4_, ...), custom_call_target="tpu_custom_call" | custom-call | tf_op jit(solution)/shard_map/step_middle/pallas_call | solution.py:258
  53.1 16.6 %apply_all.3 = (f32[24,8192]{1,0:T(8,128)}, f32[8,128]{1,0:T(8,128)}) custom-call(s32[12,32]{1,0:T(8,128)} %reshape.17.code_ref, s32[1,4,256]{2,1,0:T(4,128)} %idx_ref.3, s32[1,4]{1,0:T(1,128)} %cnt_ref.3, bf16[384,128,128]{2,1,0:T(8,128)(2,1)} %vals_ref.3, f32[24,8192]{1,0:T(8,128)} %get-tuple-element.14.blend_ref, ...), custom_call_target="tpu_custom_call" | custom-call | tf_op jit(solution)/shard_map/apply_all/pallas_call | solution.py:345
  69.7 10.6 %step_last.1 = (f32[1,128]{1,0:T(1,128)}, f32[1,128]{1,0:T(1,128)}) custom-call(f32[8,128]{1,0:T(8,128)} %get-tuple-element.18.refs_0_), custom_call_target="tpu_custom_call" | custom-call | tf_op jit(solution)/shard_map/step_last/pallas_call | solution.py:258
